TPU v7x, 256 devices: a whole 4x4x8 slice. The times are simulated.
256 devices in a mesh: anim: 16 (over y, x_lo, core), snp: 16 (over z, x_hi).
Axes of the slice: x: 4 (x_hi: 2, x_lo: 2; x = x_hi * 2 + x_lo), y: 4, z: 8, core: 2. Of those that a mesh axis runs over, the one named last changes fastest.
Arguments:
- core_geno: bfloat16 [12288, 49152], P('anim', 'snp'), may hold values from -10 to 10, as said below
- noncore_geno: bfloat16 [12288, 49152], P('anim', 'snp'), may hold values from -10 to 10, as said below
- core_inv: bfloat16 [12288, 12288], P('anim', 'snp'), may hold values from -0.0546875 to 0.0546875
- snp_effects: bfloat16 [256, 49152], P(None, 'snp'), may hold values from -0.02734375 to 0.02734375
- noncore_scale: float32 [12288], P('anim'), may hold values from 0.5 to 2
Outputs:
- noncore_out: float32 [256, 12288], P(None, 'anim')
- core_out: float32 [256, 12288], P(None, ('anim', 'snp'))
Inputs may be any that keep to these rules, and one draw needn't show every extreme that they name: `core_geno`: each column j is (c - 2 p_j) / sqrt(2 p_j (1 - p_j)) for codes c in 0, 1, 2 and a column frequency p_j shared with noncore_geno. `noncore_geno`: each column j is (c - 2 p_j) / sqrt(2 p_j (1 - p_j)) for codes c in 0, 1, 2 and a column frequency p_j shared with core_geno.
All inputs are finite; a program needn't handle non-finite values.
Results may differ from a plain program's by a relative error of at most 0.008.
Values may be sent and summed in bfloat16 or wider, within the bound.
A program may use at most 64 MiB of HBM per device.

v0:
```python
import jax
import jax.numpy as jnp
from jax import lax
from jax.sharding import PartitionSpec as P

NSNP = 49152


def contract_last(left, right):
    return lax.dot_general(
        left, right, (((1,), (1,)), ((), ())), preferred_element_type=jnp.float32
    )


def core_columns(partial_value, base, tile_cols):
    snp_index = lax.axis_index("snp")
    summed = lax.psum(partial_value, "snp")
    value = summed if base is None else base.astype(jnp.float32) - summed
    block = value.astype(jnp.bfloat16)
    whole = lax.all_gather(block, "anim", axis=1, tiled=True)
    columns = lax.dynamic_slice_in_dim(whole, snp_index * tile_cols, tile_cols, 1)
    return (block, columns)


def marker_terms(partial_value):
    total = lax.psum(partial_value, "anim")
    return (total / NSNP).astype(jnp.bfloat16)


def local(core_geno, noncore_geno, core_inv, snp_effects, noncore_scale):
    tile_cols = core_inv.shape[1]
    core_partial = contract_last(snp_effects, core_geno)
    noncore_partial = contract_last(snp_effects, noncore_geno)
    core_vals, value_cols = core_columns(core_partial, None, tile_cols)
    noncore_vals = lax.psum(noncore_partial, "snp")
    weight_partial = contract_last(value_cols, core_inv)
    core_weights = lax.psum(weight_partial, "snp").astype(jnp.bfloat16)
    snp_core = marker_terms(jnp.dot(core_weights, core_geno, preferred_element_type=jnp.float32))
    predicted = lax.psum(contract_last(snp_core, noncore_geno), "snp")
    noncore_out = noncore_scale[None, :] * (noncore_vals - predicted)
    noncore_half = noncore_out.astype(jnp.bfloat16)
    snp_noncore = marker_terms(
        jnp.dot(noncore_half, noncore_geno, preferred_element_type=jnp.float32)
    )
    back_partial = contract_last(snp_noncore, core_geno)
    core_rest, rest_cols = core_columns(back_partial, core_vals, tile_cols)
    out_partial = contract_last(rest_cols, core_inv)
    core_out = lax.psum_scatter(out_partial, "snp", scatter_dimension=1, tiled=True)
    return (noncore_out, core_out)


def solution(mesh):
    return jax.shard_map(
        local,
        mesh=mesh,
        in_specs=(P("anim", "snp"), P("anim", "snp"), P("anim", "snp"), P(None, "snp"), P("anim")),
        out_specs=(P(None, "anim"), P(None, ("anim", "snp"))),
        check_vma=False,
    )
```

profile of v0, /device:TPU:8, one launch (start us, length us, event | category | flops | bytes accessed | tf_op | source)
XLA Modules:
  0.0 1105.2 jit_solution(17298598876535657185)
XLA Ops:
  7.2 0.0 all-gather.3.cloned.1.call-start
  7.2 1.3 copy-done
  8.6 3.8 fusion.17
  12.3 89.5 %all-reduce.15 = bf16[256,768]{1,0:T(8,128)(2,1)} all-reduce(f32[256,768]{1,0:T(8,128)S(1)} %fusion.17), channel_id=1, replica_groups=mesh['anim'=16,'snp'=16] {'snp'}, use_global_device_ids=true, to_apply=%region_1.0 | all-reduce | flops 196608 | bytes 1179648 | tf_op jit(solution)/shard_map/psum | solution.py:17
  101.8 0.0 all-gather.3.cloned.1.call-update
  101.9 0.0 all-reduce.8.cloned.1.call-start
  101.9 40.4 %all-gather.3.cloned.1.call-done = bf16[256,12288]{1,0:T(8,128)(2,1)} async-done(((bf16[256,768]{1,0:T(8,128)(2,1)}), bf16[256,12288]{1,0:T(8,128)(2,1)}) %all-gather.3.cloned.1.call-update) | async-done | bytes 6291472 | tf_op jit(solution)/shard_map/all_gather | solution.py:20
  142.3 1.5 fusion.10
  143.8 87.3 %all-reduce.16 = bf16[256,768]{1,0:T(8,128)(2,1)} all-reduce(f32[256,768]{1,0:T(8,128)S(1)} %fusion.10), channel_id=1, replica_groups=mesh['anim'=16,'snp'=16] {'snp'}, use_global_device_ids=true, to_apply=%region_2.0 | all-reduce | flops 196608 | bytes 1179648 | tf_op jit(solution)/shard_map/psum | solution.py:37
  231.1 5.5 fusion.18
  236.6 0.0 all-reduce.14.cloned.1.call-start
  236.7 4.6 fusion.16
  241.3 121.1 %all-reduce.8.cloned.1.call-done = f32[256,3072]{1,0:T(8,128)} async-done(((f32[256,3072]{1,0:T(8,128)}), f32[256,3072]{1,0:T(8,128)}) %all-reduce.8.cloned.1.call-update) | async-done | bytes 3145744 | tf_op jit(solution)/shard_map/psum | solution.py:26
  362.4 5.6 fusion
  368.0 0.0 all-reduce.14.cloned.1.call-update
  368.0 0.0 all-reduce.10.cloned.1.call-start
  368.1 169.1 %all-reduce.14.cloned.1.call-done = (f32[256,768]{1,0:T(8,128)}, f32[256,768]{1,0:T(8,128)}) async-done(((f32[256,768]{1,0:T(8,128)}, f32[256,768]{1,0:T(8,128)}), (f32[256,768]{1,0:T(8,128)}, f32[256,768]{1,0:T(8,128)})) %all-reduce.14.cloned.1.call-update) | async-done | bytes 1572880 | tf_op jit(solution)/shard_map/psum | solution.py:35
  537.1 1.5 subtract_multiply_fusion
  538.6 5.7 fusion.6
  544.3 0.0 all-reduce.10.cloned.1.call-update
  544.4 0.0 all-reduce.12.cloned.1.call-start
  544.4 128.0 %all-reduce.10.cloned.1.call-done = f32[256,3072]{1,0:T(8,128)} async-done(((f32[256,3072]{1,0:T(8,128)}), f32[256,3072]{1,0:T(8,128)}) %all-reduce.10.cloned.1.call-update) | async-done | bytes 3145744 | tf_op jit(solution)/shard_map/psum | solution.py:26
  672.4 5.6 fusion.1
  678.0 0.0 all-gather.5.cloned.1.call-start
  678.0 165.4 %all-reduce.12.cloned.1.call-done = f32[256,768]{1,0:T(8,128)} async-done(((f32[256,768]{1,0:T(8,128)}), f32[256,768]{1,0:T(8,128)}) %all-reduce.12.cloned.1.call-update) | async-done | bytes 786448 | tf_op jit(solution)/shard_map/psum | solution.py:17
  843.4 1.9 subtract_convert_fusion
  845.4 0.0 all-gather.5.cloned.1.call-update
  845.4 0.0 reduce-scatter.2.cloned.1.call-start
  845.4 42.9 %all-gather.5.cloned.1.call-done = bf16[256,12288]{1,0:T(8,128)(2,1)} async-done(((bf16[256,768]{1,0:T(8,128)(2,1)}), bf16[256,12288]{1,0:T(8,128)(2,1)}) %all-gather.5.cloned.1.call-update) | async-done | bytes 6291472 | tf_op jit(solution)/shard_map/all_gather | solution.py:20
  888.4 2.4 fusion.4
  890.7 0.0 reduce-scatter.2.cloned.1.call-update
  890.8 207.5 %reduce-scatter.2.cloned.1.call-done = f32[256,48]{0,1:T(8,128)} async-done(((f32[256,768]{0,1:T(8,128)}), f32[256,48]{0,1:T(8,128)}) %reduce-scatter.2.cloned.1.call-update) | async-done | bytes 49168 | tf_op jit(solution)/shard_map/reduce_scatter | solution.py:48
  (11 shorter events, 0.1 us)
Async XLA Ops:
  7.2 1.4 copy-start
  7.2 135.1 %copy-start.2 = (bf16[768,768]{1,0:T(8,128)(2,1)S(1)}, bf16[768,768]{1,0:T(8,128)(2,1)}, u32[]{:S(2)}) copy-start(bf16[768,768]{1,0:T(8,128)(2,1)} %param.7) | copy-start | bytes 3538948
  7.2 135.1 %all-gather.3.cloned.1.call-start = ((), (), s32[]{:S(2)}) async-start(), calls=%async_computation.1 | async-start | bytes 6684672 | tf_op jit(solution)/shard_map/all_gather | solution.py:20
  101.9 260.6 %all-reduce.8.cloned.1.call-start = ((), (), s32[]{:S(2)}) async-start(), calls=%async_computation.2 | async-start | bytes 6291456 | tf_op jit(solution)/shard_map/psum | solution.py:26
  236.6 300.5 %all-reduce.14.cloned.1.call-start = ((), (), s32[]{:S(2)}) async-start(), calls=%async_computation.7 | async-start | bytes 3145728 | tf_op jit(solution)/shard_map/psum | solution.py:35
  241.3 295.8 %copy-start.4 = (f32[768]{0:T(1024)S(1)}, f32[768]{0:T(1024)}, u32[]{:S(2)}) copy-start(f32[768]{0:T(1024)} %param.9) | copy-start | bytes 9220
  368.0 304.3 %all-reduce.10.cloned.1.call-start = ((), (), s32[]{:S(2)}) async-start(), calls=%async_computation.3 | async-start | bytes 6291456 | tf_op jit(solution)/shard_map/psum | solution.py:26
  538.6 5.7 copy-start.1
  544.3 299.1 %copy-start.3 = (bf16[256,768]{1,0:T(8,128)(2,1)S(1)}, bf16[256,768]{1,0:T(8,128)(2,1)}, u32[]{:S(2)}) copy-start(bf16[256,768]{1,0:T(8,128)(2,1)} %all-reduce.15) | copy-start | bytes 1179652
  544.4 299.1 %all-reduce.12.cloned.1.call-start = ((), (), s32[]{:S(2)}) async-start(), calls=%async_computation.4 | async-start | bytes 1572864 | tf_op jit(solution)/shard_map/psum | solution.py:17
  678.0 210.4 %all-gather.5.cloned.1.call-start = ((), (), s32[]{:S(2)}) async-start(), calls=%async_computation.5 | async-start | bytes 6684672 | tf_op jit(solution)/shard_map/all_gather | solution.py:20
  845.4 252.9 %reduce-scatter.2.cloned.1.call-start = ((), (), s32[]{:S(2)}) async-start(), calls=%async_computation.6 | async-start | bytes 835584 | tf_op jit(solution)/shard_map/reduce_scatter | solution.py:48
Sparse Core Ops, SparseCore 0:
  102.0 40.2 all-gather.2
  236.8 125.6 all-reduce.7
  368.2 168.9 all-reduce.13
  544.5 127.8 all-reduce.9
  678.1 165.2 all-reduce.11
  845.5 42.8 all-gather.4
  892.8 205.5 reduce-scatter.1
where the time goes:
time: 1110 us
  waiting for transfers between devices  874 us (79%)
  blocking collectives  177 us (16%)
  matrix products  34.7 us (3%)
  between operations  14.2 us (1%)
    psum x2, waiting for transfers between devices, marker_terms(): total = lax.psum(partial_value, 'anim')  249 us
    reduce_scatter x1, waiting for transfers between devices, local(): lax.psum_scatter(out_partial, 'snp', scatter_dimension=1, tiled=True)  208 us
    psum x1, waiting for transfers between devices, local(): noncore_vals = lax.psum(noncore_partial, 'snp')  169 us
    psum x1, waiting for transfers between devices, core_columns(): summed = lax.psum(partial_value, 'snp')  165 us
    psum x1, blocking collectives, core_columns(): summed = lax.psum(partial_value, 'snp')  89.5 us
    psum x1, blocking collectives, local(): core_weights = lax.psum(weight_partial, 'snp').astype(jnp.bfloat16)  87.3 us
    all_gather x2, waiting for transfers between devices, core_columns(): whole = lax.all_gather(block, 'anim', axis=1, tiled=True)  83.3 us
    dot_general x6, matrix products, contract_last(): lax.dot_general(left, right, (((1,), (1,)), ((), ())), preferred_element_...  23.5 us
  transfers between devices with their start and end apart: 7, of which 7 were waited for; matrix products, arithmetic and copies ran while one was open for 0% of the time, Pallas kernels for 0%

commit v1 on v0

--- a/solution.py
+++ b/solution.py
@@ -34,7 +34,7 @@
     core_vals, value_cols = core_columns(core_partial, None, tile_cols)
     noncore_vals = lax.psum(noncore_partial, "snp")
     weight_partial = contract_last(value_cols, core_inv)
-    core_weights = lax.psum(weight_partial, "snp").astype(jnp.bfloat16)
+    core_weights = jnp.sum(lax.all_gather(weight_partial, "snp"), axis=0).astype(jnp.bfloat16)
     snp_core = marker_terms(jnp.dot(core_weights, core_geno, preferred_element_type=jnp.float32))
     predicted = lax.psum(contract_last(snp_core, noncore_geno), "snp")
     noncore_out = noncore_scale[None, :] * (noncore_vals - predicted)

time: 1110 us -> 1210 us (1.090)
  waiting for transfers between devices: 874 us -> 1060 us
  blocking collectives: 177 us -> 89.5 us
    all_gather x0 -> x1, waiting for transfers between devices: none -> 180 us  [local(): lax.all_gather(weight_partial, 'snp')]
    psum x1 -> x0, blocking collectives: 87.3 us -> none  [local(): core_weights = lax.psum(weight_partial, 'snp').astype(jnp.bfloat16)]
  transfers between devices with their start and end apart: 7 -> 8, of which waited for: 7 -> 8; matrix products, arithmetic and copies ran while one was open for 0% -> 0% of each run, Pallas kernels for 0% -> 0%
where the time goes in v1:
time: 1210 us
  waiting for transfers between devices  1060 us (88%)
  blocking collectives  89.5 us (7%)
  matrix products  35.5 us (3%)
  between operations  14.2 us (1%)
    psum x2, waiting for transfers between devices, marker_terms(): total = lax.psum(partial_value, 'anim')  250 us
    reduce_scatter x1, waiting for transfers between devices, local(): lax.psum_scatter(out_partial, 'snp', scatter_dimension=1, tiled=True)  208 us
    all_gather x1, waiting for transfers between devices, local(): lax.all_gather(weight_partial, 'snp')  180 us
    psum x1, waiting for transfers between devices, local(): noncore_vals = lax.psum(noncore_partial, 'snp')  169 us
    psum x1, waiting for transfers between devices, core_columns(): summed = lax.psum(partial_value, 'snp')  165 us
    psum x1, blocking collectives, core_columns(): summed = lax.psum(partial_value, 'snp')  89.5 us
    all_gather x2, waiting for transfers between devices, core_columns(): whole = lax.all_gather(block, 'anim', axis=1, tiled=True)  83.3 us
    dot_general x6, matrix products, contract_last(): lax.dot_general(left, right, (((1,), (1,)), ((), ())), preferred_element_...  24.4 us
  transfers between devices with their start and end apart: 8, of which 8 were waited for; matrix products, arithmetic and copies ran while one was open for 0% of the time, Pallas kernels for 0%

profile of v1, /device:TPU:8, one launch (start us, length us, event | category | flops | bytes accessed | tf_op | source)
XLA Modules:
  0.0 1205.2 jit_solution(3200015114970236088)
XLA Ops:
  7.2 0.0 all-gather.5.cloned.1.call-start
  7.2 1.3 copy-done
  8.6 3.8 fusion.17
  12.3 89.5 %all-reduce.14 = bf16[256,768]{1,0:T(8,128)(2,1)} all-reduce(f32[256,768]{1,0:T(8,128)S(1)} %fusion.17), channel_id=1, replica_groups=mesh['anim'=16,'snp'=16] {'snp'}, use_global_device_ids=true, to_apply=%region_1.0 | all-reduce | flops 196608 | bytes 1179648 | tf_op jit(solution)/shard_map/psum | solution.py:17
  101.8 0.0 all-gather.5.cloned.1.call-update
  101.9 0.0 all-gather.9.cloned.1.call-start
  101.9 40.4 %all-gather.5.cloned.1.call-done = bf16[256,12288]{1,0:T(8,128)(2,1)} async-done(((bf16[256,768]{1,0:T(8,128)(2,1)}), bf16[256,12288]{1,0:T(8,128)(2,1)}) %all-gather.5.cloned.1.call-update) | async-done | bytes 6291472 | tf_op jit(solution)/shard_map/all_gather | solution.py:20
  142.3 2.4 fusion.10
  144.6 0.0 all-gather.9.cloned.1.call-update
  144.7 0.0 all-reduce.7.cloned.1.call-start
  144.7 180.1 %all-gather.9.cloned.1.call-done = f32[4096,768]{1,0:T(8,128)} async-done(((f32[256,768]{1,0:T(8,128)}), f32[4096,768]{1,0:T(8,128)}) %all-gather.9.cloned.1.call-update) | async-done | bytes 12582928 | tf_op jit(solution)/shard_map/all_gather | solution.py:37
  324.8 5.4 reduce_sum.9
  330.1 5.4 fusion.18
  335.6 0.0 all-reduce.13.cloned.1.call-start
  335.6 4.6 fusion.16
  340.3 122.2 %all-reduce.7.cloned.1.call-done = f32[256,3072]{1,0:T(8,128)} async-done(((f32[256,3072]{1,0:T(8,128)}), f32[256,3072]{1,0:T(8,128)}) %all-reduce.7.cloned.1.call-update) | async-done | bytes 3145744 | tf_op jit(solution)/shard_map/psum | solution.py:26
  462.5 5.6 fusion
  468.1 0.0 all-reduce.9.cloned.1.call-start
  468.1 169.0 %all-reduce.13.cloned.1.call-done = (f32[256,768]{1,0:T(8,128)}, f32[256,768]{1,0:T(8,128)}) async-done(((f32[256,768]{1,0:T(8,128)}, f32[256,768]{1,0:T(8,128)}), (f32[256,768]{1,0:T(8,128)}, f32[256,768]{1,0:T(8,128)})) %all-reduce.13.cloned.1.call-update) | async-done | bytes 1572880 | tf_op jit(solution)/shard_map/psum | solution.py:35
  637.2 1.5 subtract_multiply_fusion
  638.6 5.7 fusion.6
  644.3 0.0 all-reduce.9.cloned.1.call-update
  644.4 0.0 all-reduce.11.cloned.1.call-start
  644.4 127.9 %all-reduce.9.cloned.1.call-done = f32[256,3072]{1,0:T(8,128)} async-done(((f32[256,3072]{1,0:T(8,128)}), f32[256,3072]{1,0:T(8,128)}) %all-reduce.9.cloned.1.call-update) | async-done | bytes 3145744 | tf_op jit(solution)/shard_map/psum | solution.py:26
  772.3 5.6 fusion.1
  778.0 0.0 all-gather.7.cloned.1.call-start
  778.0 165.4 %all-reduce.11.cloned.1.call-done = f32[256,768]{1,0:T(8,128)} async-done(((f32[256,768]{1,0:T(8,128)}), f32[256,768]{1,0:T(8,128)}) %all-reduce.11.cloned.1.call-update) | async-done | bytes 786448 | tf_op jit(solution)/shard_map/psum | solution.py:17
  943.4 2.0 subtract_convert_fusion
  945.4 0.0 reduce-scatter.2.cloned.1.call-start
  945.5 42.9 %all-gather.7.cloned.1.call-done = bf16[256,12288]{1,0:T(8,128)(2,1)} async-done(((bf16[256,768]{1,0:T(8,128)(2,1)}), bf16[256,12288]{1,0:T(8,128)(2,1)}) %all-gather.7.cloned.1.call-update) | async-done | bytes 6291472 | tf_op jit(solution)/shard_map/all_gather | solution.py:20
  988.4 2.4 fusion.4
  990.8 207.5 %reduce-scatter.2.cloned.1.call-done = f32[256,48]{0,1:T(8,128)} async-done(((f32[256,768]{0,1:T(8,128)}), f32[256,48]{0,1:T(8,128)}) %reduce-scatter.2.cloned.1.call-update) | async-done | bytes 49168 | tf_op jit(solution)/shard_map/reduce_scatter | solution.py:48
  (14 shorter events, 0.1 us)
Async XLA Ops:
  7.2 1.4 copy-start
  7.2 135.1 %copy-start.2 = (bf16[768,768]{1,0:T(8,128)(2,1)S(1)}, bf16[768,768]{1,0:T(8,128)(2,1)}, u32[]{:S(2)}) copy-start(bf16[768,768]{1,0:T(8,128)(2,1)} %param.7) | copy-start | bytes 3538948
  7.2 135.1 %all-gather.5.cloned.1.call-start = ((), (), s32[]{:S(2)}) async-start(), calls=%async_computation.1 | async-start | bytes 6684672 | tf_op jit(solution)/shard_map/all_gather | solution.py:20
  101.9 222.9 %all-gather.9.cloned.1.call-start = ((), (), s32[]{:S(2)}) async-start(), calls=%async_computation.7 | async-start | bytes 13369344 | tf_op jit(solution)/shard_map/all_gather | solution.py:37
  144.7 317.8 %all-reduce.7.cloned.1.call-start = ((), (), s32[]{:S(2)}) async-start(), calls=%async_computation.2 | async-start | bytes 6291456 | tf_op jit(solution)/shard_map/psum | solution.py:26
  335.6 301.6 %all-reduce.13.cloned.1.call-start = ((), (), s32[]{:S(2)}) async-start(), calls=%async_computation.8 | async-start | bytes 3145728 | tf_op jit(solution)/shard_map/psum | solution.py:35
  340.3 296.9 %copy-start.4 = (f32[768]{0:T(1024)S(1)}, f32[768]{0:T(1024)}, u32[]{:S(2)}) copy-start(f32[768]{0:T(1024)} %param.9) | copy-start | bytes 9220
  468.1 304.3 %all-reduce.9.cloned.1.call-start = ((), (), s32[]{:S(2)}) async-start(), calls=%async_computation.3 | async-start | bytes 6291456 | tf_op jit(solution)/shard_map/psum | solution.py:26
  638.6 5.7 copy-start.1
  644.4 299.1 %copy-start.3 = (bf16[256,768]{1,0:T(8,128)(2,1)S(1)}, bf16[256,768]{1,0:T(8,128)(2,1)}, u32[]{:S(2)}) copy-start(bf16[256,768]{1,0:T(8,128)(2,1)} %all-reduce.14) | copy-start | bytes 1179652
  644.4 299.0 %all-reduce.11.cloned.1.call-start = ((), (), s32[]{:S(2)}) async-start(), calls=%async_computation.4 | async-start | bytes 1572864 | tf_op jit(solution)/shard_map/psum | solution.py:17
  778.0 210.4 %all-gather.7.cloned.1.call-start = ((), (), s32[]{:S(2)}) async-start(), calls=%async_computation.5 | async-start | bytes 6684672 | tf_op jit(solution)/shard_map/all_gather | solution.py:20
  945.4 252.9 %reduce-scatter.2.cloned.1.call-start = ((), (), s32[]{:S(2)}) async-start(), calls=%async_computation.6 | async-start | bytes 835584 | tf_op jit(solution)/shard_map/reduce_scatter | solution.py:48
Sparse Core Ops, SparseCore 0:
  102.0 40.2 all-gather.4
  145.4 179.3 all-gather.8
  335.7 126.7 all-reduce.6
  468.2 168.9 all-reduce.12
  644.5 127.8 all-reduce.8
  778.1 165.2 all-reduce.10
  945.5 42.8 all-gather.6
  992.8 205.5 reduce-scatter.1

commit v2 on v0

--- a/solution.py
+++ b/solution.py
@@ -17,7 +17,9 @@
     summed = lax.psum(partial_value, "snp")
     value = summed if base is None else base.astype(jnp.float32) - summed
     block = value.astype(jnp.bfloat16)
-    whole = lax.all_gather(block, "anim", axis=1, tiled=True)
+    whole = jnp.concatenate(
+        lax.all_to_all(jnp.stack([block] * lax.axis_size("anim")), "anim", 0, 0), axis=1
+    )
     columns = lax.dynamic_slice_in_dim(whole, snp_index * tile_cols, tile_cols, 1)
     return (block, columns)
 

time: 1110 us -> 1170 us (1.054)
  blocking collectives: 177 us -> 246 us
  waiting for transfers between devices: 874 us -> 859 us
    all_gather x2 -> x0, waiting for transfers between devices: 83.3 us -> none  [core_columns(): whole = lax.all_gather(block, 'anim', axis=1, tiled=True)]
    all_to_all x0 -> x1, blocking collectives: none -> 75.2 us  [core_columns(): lax.all_to_all(jnp.stack([block] * lax.axis_size('anim')), 'anim', 0, 0)]
    all_to_all x0 -> x1, waiting for transfers between devices: none -> 71.2 us  [core_columns(): lax.all_to_all(jnp.stack([block] * lax.axis_size('anim')), 'anim', 0, 0)]
  transfers between devices with their start and end apart: 7 -> 6, of which waited for: 7 -> 6; matrix products, arithmetic and copies ran while one was open for 0% -> 0% of each run, Pallas kernels for 0% -> 0%
where the time goes in v2:
time: 1170 us
  waiting for transfers between devices  859 us (73%)
  blocking collectives  246 us (21%)
  matrix products  33.7 us (3%)
  between operations  13.9 us (1%)
    psum x2, waiting for transfers between devices, marker_terms(): total = lax.psum(partial_value, 'anim')  251 us
    reduce_scatter x1, waiting for transfers between devices, local(): lax.psum_scatter(out_partial, 'snp', scatter_dimension=1, tiled=True)  203 us
    psum x1, waiting for transfers between devices, local(): noncore_vals = lax.psum(noncore_partial, 'snp')  169 us
    psum x1, waiting for transfers between devices, core_columns(): summed = lax.psum(partial_value, 'snp')  165 us
    psum x1, blocking collectives, core_columns(): summed = lax.psum(partial_value, 'snp')  89 us
    psum x1, blocking collectives, local(): core_weights = lax.psum(weight_partial, 'snp').astype(jnp.bfloat16)  82.3 us
    all_to_all x1, blocking collectives, core_columns(): lax.all_to_all(jnp.stack([block] * lax.axis_size('anim')), 'anim', 0, 0)  75.2 us
    all_to_all x1, waiting for transfers between devices, core_columns(): lax.all_to_all(jnp.stack([block] * lax.axis_size('anim')), 'anim', 0, 0)  71.2 us
  transfers between devices with their start and end apart: 6, of which 6 were waited for; matrix products, arithmetic and copies ran while one was open for 0% of the time, Pallas kernels for 0%

profile of v2, /device:TPU:8, one launch (start us, length us, event | category | flops | bytes accessed | tf_op | source)
XLA Modules:
  0.0 1168.0 jit_solution(14101851491667162387)
XLA Ops:
  7.2 1.4 copy-done
  8.6 3.7 fusion.17
  12.3 89.0 %all-reduce.15 = bf16[256,768]{1,0:T(8,128)(2,1)S(1)} all-reduce(f32[256,768]{1,0:T(8,128)S(1)} %fusion.17), channel_id=1, replica_groups=mesh['anim'=16,'snp'=16] {'snp'}, use_global_device_ids=true, to_apply=%region_1.0 | all-reduce | flops 196608 | bytes 1179648 | tf_op jit(solution)/shard_map/psum | solution.py:17
  101.4 0.2 copy.7
  101.6 0.6 copy-done.3
  102.1 3.3 stack.4
  105.4 5.7 all-to-all-start
  111.1 0.0 all-reduce.8.cloned.1.call-start
  111.1 71.2 %all-to-all-done = bf16[16,256,768]{1,2,0:T(8,128)(2,1)} async-done(((bf16[16,256,768]{1,2,0:T(8,128)(2,1)}), bf16[16,256,768]{1,2,0:T(8,128)(2,1)}, u32[]{:S(2)}, u32[]{:S(2)}) %all-to-all-start) | async-done | bytes 6291488 | tf_op jit(solution)/shard_map/all_to_all | solution.py:21
  182.3 1.5 fusion.10
  183.8 82.3 %all-reduce.16 = bf16[256,768]{1,0:T(8,128)(2,1)} all-reduce(f32[256,768]{1,0:T(8,128)S(1)} %fusion.10), channel_id=1, replica_groups=mesh['anim'=16,'snp'=16] {'snp'}, use_global_device_ids=true, to_apply=%region_2.0 | all-reduce | flops 196608 | bytes 1179648 | tf_op jit(solution)/shard_map/psum | solution.py:39
  266.1 5.5 fusion.18
  271.7 0.0 all-reduce.14.cloned.1.call-start
  271.7 4.6 fusion.16
  276.4 123.2 %all-reduce.8.cloned.1.call-done = f32[256,3072]{1,0:T(8,128)} async-done(((f32[256,3072]{1,0:T(8,128)}), f32[256,3072]{1,0:T(8,128)}) %all-reduce.8.cloned.1.call-update) | async-done | bytes 3145744 | tf_op jit(solution)/shard_map/psum | solution.py:28
  399.6 5.6 fusion
  405.2 0.0 all-reduce.10.cloned.1.call-start
  405.2 169.0 %all-reduce.14.cloned.1.call-done = (f32[256,768]{1,0:T(8,128)}, f32[256,768]{1,0:T(8,128)}) async-done(((f32[256,768]{1,0:T(8,128)}, f32[256,768]{1,0:T(8,128)}), (f32[256,768]{1,0:T(8,128)}, f32[256,768]{1,0:T(8,128)})) %all-reduce.14.cloned.1.call-update) | async-done | bytes 1572880 | tf_op jit(solution)/shard_map/psum | solution.py:37
  574.3 1.5 subtract_multiply_fusion
  575.8 5.7 fusion.6
  581.4 0.0 all-reduce.10.cloned.1.call-update
  581.5 0.0 all-reduce.12.cloned.1.call-start
  581.5 127.6 %all-reduce.10.cloned.1.call-done = f32[256,3072]{1,0:T(8,128)} async-done(((f32[256,3072]{1,0:T(8,128)}), f32[256,3072]{1,0:T(8,128)}) %all-reduce.10.cloned.1.call-update) | async-done | bytes 3145744 | tf_op jit(solution)/shard_map/psum | solution.py:28
  709.1 5.6 fusion.1
  714.7 0.0 reduce-scatter.2.cloned.1.call-start
  714.8 165.4 %all-reduce.12.cloned.1.call-done = f32[256,768]{1,0:T(8,128)} async-done(((f32[256,768]{1,0:T(8,128)}), f32[256,768]{1,0:T(8,128)}) %all-reduce.12.cloned.1.call-update) | async-done | bytes 786448 | tf_op jit(solution)/shard_map/psum | solution.py:17
  880.1 1.2 subtract_convert_fusion
  881.4 0.2 copy.8
  881.5 0.6 stack.5
  882.1 75.2 %all_to_all.10 = bf16[16,256,768]{1,2,0:T(8,128)(2,1)S(1)} all-to-all(bf16[16,256,768]{1,2,0:T(8,128)(2,1)S(1)} %stack.5), channel_id=1, replica_groups=mesh['anim'=16,'snp'=16] {'anim'}, dimensions={0} | all-to-all | bytes 12582912 | tf_op jit(solution)/shard_map/all_to_all | solution.py:21
  957.3 1.4 fusion.4
  958.7 202.8 %reduce-scatter.2.cloned.1.call-done = f32[256,48]{0,1:T(8,128)} async-done(((f32[256,768]{0,1:T(8,128)}), f32[256,48]{0,1:T(8,128)}) %reduce-scatter.2.cloned.1.call-update) | async-done | bytes 49168 | tf_op jit(solution)/shard_map/reduce_scatter | solution.py:50
  (14 shorter events, 0.1 us)
Async XLA Ops:
  7.2 1.4 copy-start
  101.4 0.8 copy-start.3
  105.4 77.0 %copy-start.2 = (bf16[768,768]{1,0:T(8,128)(2,1)S(1)}, bf16[768,768]{1,0:T(8,128)(2,1)}, u32[]{:S(2)}) copy-start(bf16[768,768]{1,0:T(8,128)(2,1)} %param.7) | copy-start | bytes 3538948
  105.4 77.0 %all-to-all-start = ((bf16[16,256,768]{1,2,0:T(8,128)(2,1)}), bf16[16,256,768]{1,2,0:T(8,128)(2,1)}, u32[]{:S(2)}, u32[]{:S(2)}) async-start(bf16[16,256,768]{1,2,0:T(8,128)(2,1)} %stack.4), calls=%async_computation | async-start | bytes 12582912 | tf_op jit(solution)/shard_map/all_to_all | solution.py:21
  111.1 288.5 %all-reduce.8.cloned.1.call-start = ((), (), s32[]{:S(2)}) async-start(), calls=%async_computation.3 | async-start | bytes 6291456 | tf_op jit(solution)/shard_map/psum | solution.py:28
  271.7 302.6 %all-reduce.14.cloned.1.call-start = ((), (), s32[]{:S(2)}) async-start(), calls=%async_computation.7 | async-start | bytes 3145728 | tf_op jit(solution)/shard_map/psum | solution.py:37
  276.4 297.9 %copy-start.5 = (f32[768]{0:T(1024)S(1)}, f32[768]{0:T(1024)}, u32[]{:S(2)}) copy-start(f32[768]{0:T(1024)} %param.9) | copy-start | bytes 9220
  405.2 303.9 %all-reduce.10.cloned.1.call-start = ((), (), s32[]{:S(2)}) async-start(), calls=%async_computation.4 | async-start | bytes 6291456 | tf_op jit(solution)/shard_map/psum | solution.py:28
  575.7 5.7 copy-start.1
  581.5 298.7 %copy-start.4 = (bf16[256,768]{1,0:T(8,128)(2,1)S(1)}, bf16[256,768]{1,0:T(8,128)(2,1)}, u32[]{:S(2)}) copy-start(bf16[256,768]{1,0:T(8,128)(2,1)} %copy-done.3) | copy-start | bytes 1179652
  581.5 298.7 %all-reduce.12.cloned.1.call-start = ((), (), s32[]{:S(2)}) async-start(), calls=%async_computation.5 | async-start | bytes 1572864 | tf_op jit(solution)/shard_map/psum | solution.py:17
  714.7 446.8 %reduce-scatter.2.cloned.1.call-start = ((), (), s32[]{:S(2)}) async-start(), calls=%async_computation.6 | async-start | bytes 835584 | tf_op jit(solution)/shard_map/reduce_scatter | solution.py:50
Sparse Core Ops, SparseCore 0:
  271.8 127.7 all-reduce.7
  405.3 168.9 all-reduce.13
  581.6 127.4 all-reduce.9
  714.8 165.2 all-reduce.11
  958.8 202.6 reduce-scatter.1
